TPU v7x, 32 devices: a whole 2x2x4 slice. The times are simulated.
32 devices in a mesh: tok: 16 (over z, y, x), hd: 2 (over core).
Axes of the slice: x: 2, y: 2, z: 4, core: 2. Of those that a mesh axis runs over, the one named last changes fastest.
Arguments:
- hidden_in: bfloat16 [16384, 768], P(('tok', 'hd')), may hold values from -6 to 6
- norm_gains: bfloat16 [2, 768], P(None, ('tok', 'hd')), may hold values from 0.099609375 to 1.8984375
- w_qkv: bfloat16 [2304, 768], P(('tok', 'hd')), may hold values from -0.21875 to 0.21875
- w_attn_out: bfloat16 [768, 768], P(('tok', 'hd')), may hold values from -1.75 to 1.75
- w_in: bfloat16 [2304, 768], P(('tok', 'hd')), may hold values from -0.21875 to 0.21875
- w_down: bfloat16 [768, 1152], P(('tok', 'hd')), may hold values from -0.1875 to 0.1875
- cotangent: bfloat16 [16384, 768], P(('tok', 'hd')), may hold values from -6 to 6
- segment_ids: int32 [16384], P(('tok', 'hd')), may hold values from 0 to 31, as said below
- row_counts: int32 [32], P(('tok', 'hd')), may hold values from 256 to 512, as said below
Outputs:
- output: bfloat16 [16384, 768], P(('tok', 'hd'))
- input_grad: bfloat16 [16384, 768], P(('tok', 'hd'))
- grad_qkv: float32 [2304, 768], P(('tok', 'hd'))
- grad_attn_out: float32 [768, 768], P(('tok', 'hd'))
- grad_in: float32 [2304, 768], P(('tok', 'hd'))
- grad_down: float32 [768, 1152], P(('tok', 'hd'))
- grad_gains: float32 [2, 768], P(None, ('tok', 'hd'))
Inputs may be any that keep to these rules, and one draw needn't show every extreme that they name: `segment_ids`: within each group of 1024 rows the ids start at 0 and never fall; a document is a run of rows with one id; documents begin only at rows whose index within the group is a multiple of 32, and always at rows whose index within a block is 256, so a document may span two blocks of a group. In every draw some group holds 32 documents. `row_counts`: rows of a block at or beyond its count are padding.
All inputs are finite; a program needn't handle non-finite values.
Results may differ from a plain program's by a relative error of at most 0.015.
Values may be sent and summed in bfloat16 or wider, within the bound.
A program may use at most 192 MiB of HBM per device.

v0:
```python
import math
import jax
import jax.numpy as jnp
from jax import lax
from jax.sharding import PartitionSpec as P

HEADS = 12
HEAD_DIM = 64
EPS = 1e-05
THETA = 160000.0
NEG = -1e30


def layer_norm(row_values, gain):
    mean_value = jnp.mean(row_values, axis=-1, keepdims=True)
    centred = row_values - mean_value
    variance = jnp.mean(centred * centred, axis=-1, keepdims=True)
    return centred * lax.rsqrt(variance + EPS) * gain


def doc_positions(seg_ids):
    row_index = jnp.arange(seg_ids.shape[0], dtype=jnp.int32)
    begins = jnp.concatenate([jnp.ones((1,), dtype=jnp.bool_), seg_ids[1:] != seg_ids[:-1]])
    first_row = lax.cummax(jnp.where(begins, row_index, 0), axis=0)
    return (row_index - first_row).astype(jnp.float32)


def rotary_tables(position, head_size):
    half_size = head_size // 2
    freqs = THETA ** (-jnp.arange(half_size, dtype=jnp.float32) * 2.0 / head_size)
    angles = position[:, None] * freqs[None, :]
    angles = jnp.concatenate([angles, angles], axis=1)
    return (jnp.cos(angles), jnp.sin(angles))


def rotate(head_values, cos_table, sin_table):
    half_size = head_values.shape[-1] // 2
    turned = jnp.concatenate([-head_values[..., half_size:], head_values[..., :half_size]], axis=-1)
    return head_values * cos_table[:, None, :] + turned * sin_table[:, None, :]


def times_t(left, right):
    return lax.dot_general(
        left, right, (((1,), (1,)), ((), ())), preferred_element_type=jnp.float32
    )


def outer_sum(left, right):
    return lax.dot_general(
        left, right, (((0,), (0,)), ((), ())), preferred_element_type=jnp.float32
    )


def times(left, right):
    return jnp.dot(left, right, preferred_element_type=jnp.float32)


def gated(gate, up_part):
    return jax.nn.gelu(gate, approximate=False) * up_part


def block_scores(queries, keys, seg_ids, ok_rows, first_row, block_size):
    query_block = lax.dynamic_slice_in_dim(queries, first_row, block_size, 0)
    seg_query = lax.dynamic_slice_in_dim(seg_ids, first_row, block_size, 0)
    ok_query = lax.dynamic_slice_in_dim(ok_rows, first_row, block_size, 0)
    query_index = first_row + jnp.arange(block_size, dtype=jnp.int32)
    key_index = jnp.arange(seg_ids.shape[0], dtype=jnp.int32)
    same_doc = (seg_query[:, None] == seg_ids[None, :]) & ok_query[:, None] & ok_rows[None, :]
    allowed = same_doc | (query_index[:, None] == key_index[None, :])
    scores = (
        jnp.einsum("qhd,khd->hqk", query_block, keys, preferred_element_type=jnp.float32) * 0.125
    )
    return (query_block, allowed, jnp.where(allowed[None], scores, NEG))


def attend_forward(queries, keys, values, seg_ids, ok_rows, block_size):

    def one_block(block_index):
        first_row = block_index * block_size
        _, _, masked = block_scores(queries, keys, seg_ids, ok_rows, first_row, block_size)
        top_score = jnp.max(masked, axis=-1, keepdims=True)
        weights_exp = jnp.exp(masked - top_score)
        total = jnp.sum(weights_exp, axis=-1, keepdims=True)
        probs = (weights_exp / total).astype(jnp.bfloat16)
        mixed = jnp.einsum("hqk,khd->qhd", probs, values, preferred_element_type=jnp.float32)
        return (mixed.astype(jnp.bfloat16), (top_score + jnp.log(total))[..., 0])

    block_ids = jnp.arange(queries.shape[0] // block_size, dtype=jnp.int32)
    mixed, log_totals = lax.map(one_block, block_ids)
    return (mixed.reshape(queries.shape), log_totals)


def attend_backward(queries, keys, values, grad_mixed, log_totals, seg_ids, ok_rows, block_size):

    def one_block(carry, inputs_here):
        grad_keys, grad_values = carry
        block_index, log_total = inputs_here
        first_row = block_index * block_size
        query_block, allowed, masked = block_scores(
            queries, keys, seg_ids, ok_rows, first_row, block_size
        )
        probs = jnp.exp(masked - log_total[..., None])
        probs_low = probs.astype(jnp.bfloat16)
        grad_block = lax.dynamic_slice_in_dim(grad_mixed, first_row, block_size, 0)
        grad_probs = jnp.einsum(
            "qhd,khd->hqk", grad_block, values, preferred_element_type=jnp.float32
        )
        inner = jnp.sum(probs * grad_probs, axis=-1, keepdims=True)
        grad_scores = jnp.where(allowed[None], probs * (grad_probs - inner), 0.0).astype(
            jnp.bfloat16
        )
        grad_query = (
            jnp.einsum("hqk,khd->qhd", grad_scores, keys, preferred_element_type=jnp.float32)
            * 0.125
        )
        grad_keys = (
            grad_keys
            + jnp.einsum(
                "hqk,qhd->khd", grad_scores, query_block, preferred_element_type=jnp.float32
            )
            * 0.125
        )
        grad_values = grad_values + jnp.einsum(
            "hqk,qhd->khd", probs_low, grad_block, preferred_element_type=jnp.float32
        )
        return ((grad_keys, grad_values), grad_query.astype(jnp.bfloat16))

    zero_grads = jnp.zeros(keys.shape, jnp.float32)
    block_ids = jnp.arange(queries.shape[0] // block_size, dtype=jnp.int32)
    (grad_keys, grad_values), grad_query = lax.scan(
        one_block, (zero_grads, zero_grads), (block_ids, log_totals)
    )
    return (
        grad_query.reshape(queries.shape),
        grad_keys.astype(jnp.bfloat16),
        grad_values.astype(jnp.bfloat16),
    )


def per_device(
    hidden_in, norm_gains, w_qkv, w_attn_out, w_in, w_down, cotangent, segment_ids, row_counts
):
    row_total, width = hidden_in.shape
    group_count = lax.axis_size("hd")
    heads_here = HEADS // group_count
    part_width = width // group_count
    group_rows = group_count * row_total
    block_size = min(512, group_rows)
    ff_width = w_down.shape[1]
    gathered = (
        lax.all_gather(w_qkv, ("tok", "hd"), axis=0, tiled=True),
        lax.all_gather(w_attn_out, ("tok", "hd"), axis=0, tiled=True),
        lax.all_gather(w_in, ("tok", "hd"), axis=0, tiled=True),
        lax.all_gather(w_down, ("tok", "hd"), axis=0, tiled=True),
        lax.all_gather(norm_gains, ("tok", "hd"), axis=1, tiled=True),
    )
    full_qkv, full_attn_out, full_in, full_down, full_gains = gathered
    gain_attn = full_gains[0].astype(jnp.float32)
    gain_mlp = full_gains[1].astype(jnp.float32)
    row_index = jnp.arange(row_total, dtype=jnp.int32)
    keep_rows = (row_index < row_counts[0]).astype(jnp.float32)[:, None]
    seg_pair, count_pair = (
        lax.all_gather(segment_ids, "hd", axis=0, tiled=True),
        lax.all_gather(row_counts, "hd", axis=0, tiled=True),
    )
    ok_pair = jnp.concatenate([row_index < count_pair[anchor] for anchor in range(group_count)])
    group_positions = doc_positions(seg_pair)
    own_start = lax.axis_index("hd") * row_total
    own_positions = lax.dynamic_slice_in_dim(group_positions, own_start, row_total, 0)
    cos_table, sin_table = rotary_tables(own_positions, HEAD_DIM)
    wide_in = hidden_in.astype(jnp.float32)
    normed_f, attn_norm_pull = jax.vjp(layer_norm, wide_in, gain_attn)
    normed1 = normed_f.astype(jnp.bfloat16)
    qkv = times_t(normed1, full_qkv)
    q_rot = rotate(qkv[:, :width].reshape(row_total, HEADS, HEAD_DIM), cos_table, sin_table)
    k_rot = rotate(
        qkv[:, width : 2 * width].reshape(row_total, HEADS, HEAD_DIM), cos_table, sin_table
    )
    packed = jnp.concatenate(
        [q_rot.reshape(row_total, width), k_rot.reshape(row_total, width), qkv[:, 2 * width :]],
        axis=1,
    ).astype(jnp.bfloat16)
    packed = packed.reshape(row_total, 3, group_count, part_width)
    head_rows = lax.all_to_all(packed, "hd", split_axis=2, concat_axis=0, tiled=True)
    q_heads = head_rows[:, 0, 0].reshape(group_rows, heads_here, HEAD_DIM)
    k_heads = head_rows[:, 1, 0].reshape(group_rows, heads_here, HEAD_DIM)
    v_heads = head_rows[:, 2, 0].reshape(group_rows, heads_here, HEAD_DIM)
    mixed, log_totals = attend_forward(q_heads, k_heads, v_heads, seg_pair, ok_pair, block_size)
    mixed_heads = mixed.reshape(group_rows, 1, part_width)
    attended = lax.all_to_all(mixed_heads, "hd", split_axis=0, concat_axis=1, tiled=True).reshape(
        row_total, width
    )
    residual = wide_in + keep_rows * times_t(attended, full_attn_out)
    normed_g, mlp_norm_pull = jax.vjp(layer_norm, residual, gain_mlp)
    normed2 = normed_g.astype(jnp.bfloat16)
    both_parts = times_t(normed2, full_in)
    hidden_f, gate_pull = jax.vjp(gated, both_parts[:, :ff_width], both_parts[:, ff_width:])
    hidden = hidden_f.astype(jnp.bfloat16)
    output = (residual + keep_rows * times_t(hidden, full_down)).astype(jnp.bfloat16)
    back_weights = (
        lax.all_gather(w_qkv, ("tok", "hd"), axis=0, tiled=True),
        lax.all_gather(w_attn_out, ("tok", "hd"), axis=0, tiled=True),
        lax.all_gather(w_in, ("tok", "hd"), axis=0, tiled=True),
        lax.all_gather(w_down, ("tok", "hd"), axis=0, tiled=True),
        lax.all_gather(norm_gains, ("tok", "hd"), axis=1, tiled=True),
    )
    back_qkv, back_attn_out, back_in, back_down, _ = back_weights
    grad_out_rows = cotangent.astype(jnp.float32)
    grad_branch2 = (keep_rows * grad_out_rows).astype(jnp.bfloat16)
    down_term = outer_sum(grad_branch2, hidden)
    grad_hidden = times(grad_branch2, back_down)
    grad_gate, grad_up = gate_pull(grad_hidden)
    grad_both = jnp.concatenate([grad_gate, grad_up], axis=1).astype(jnp.bfloat16)
    in_term = outer_sum(grad_both, normed2)
    grad_normed2 = times(grad_both, back_in)
    grad_res_norm, gain_mlp_term = mlp_norm_pull(grad_normed2)
    grad_residual = grad_out_rows + grad_res_norm
    grad_branch1 = (keep_rows * grad_residual).astype(jnp.bfloat16)
    attn_out_term = outer_sum(grad_branch1, attended)
    grad_attended = times(grad_branch1, back_attn_out).astype(jnp.bfloat16)
    grad_heads = lax.all_to_all(
        grad_attended.reshape(row_total, group_count, part_width),
        "hd",
        split_axis=1,
        concat_axis=0,
        tiled=True,
    )
    grad_heads = grad_heads.reshape(group_rows, heads_here, HEAD_DIM)
    grad_query, grad_keys, grad_values = attend_backward(
        q_heads, k_heads, v_heads, grad_heads, log_totals, seg_pair, ok_pair, block_size
    )
    grad_stack = jnp.stack(
        [
            grad_query.reshape(group_rows, part_width),
            grad_keys.reshape(group_rows, part_width),
            grad_values.reshape(group_rows, part_width),
        ],
        axis=1,
    )
    grad_stack = grad_stack.reshape(group_rows, 3, 1, part_width)
    grad_rows = lax.all_to_all(grad_stack, "hd", split_axis=0, concat_axis=2, tiled=True).reshape(
        row_total, 3, width
    )
    grad_q = rotate(
        grad_rows[:, 0].astype(jnp.float32).reshape(row_total, HEADS, HEAD_DIM),
        cos_table,
        -sin_table,
    )
    grad_k = rotate(
        grad_rows[:, 1].astype(jnp.float32).reshape(row_total, HEADS, HEAD_DIM),
        cos_table,
        -sin_table,
    )
    grad_qkv = jnp.concatenate(
        [
            grad_q.reshape(row_total, width).astype(jnp.bfloat16),
            grad_k.reshape(row_total, width).astype(jnp.bfloat16),
            grad_rows[:, 2],
        ],
        axis=1,
    )
    qkv_term = outer_sum(grad_qkv, normed1)
    grad_normed1 = times(grad_qkv, back_qkv)
    grad_in_norm, gain_attn_term = attn_norm_pull(grad_normed1)
    input_grad = (grad_residual + grad_in_norm).astype(jnp.bfloat16)
    gain_terms = jnp.stack([gain_attn_term, gain_mlp_term])
    sum_qkv, sum_attn_out, sum_in, sum_down, sum_gains = (
        lax.psum_scatter(qkv_term, ("tok", "hd"), scatter_dimension=0, tiled=True),
        lax.psum_scatter(attn_out_term, ("tok", "hd"), scatter_dimension=0, tiled=True),
        lax.psum_scatter(in_term, ("tok", "hd"), scatter_dimension=0, tiled=True),
        lax.psum_scatter(down_term, ("tok", "hd"), scatter_dimension=0, tiled=True),
        lax.psum_scatter(gain_terms, ("tok", "hd"), scatter_dimension=1, tiled=True),
    )
    token_total = row_total * lax.axis_size("tok") * lax.axis_size("hd")
    scale = 1.0 / math.sqrt(token_total)
    return (
        output,
        input_grad,
        sum_qkv * scale,
        sum_attn_out * scale,
        sum_in * scale,
        sum_down * scale,
        sum_gains * scale,
    )


def solution(mesh):
    return jax.shard_map(
        per_device,
        mesh=mesh,
        in_specs=(
            P(("tok", "hd"), None),
            P(None, ("tok", "hd")),
            P(("tok", "hd"), None),
            P(("tok", "hd"), None),
            P(("tok", "hd"), None),
            P(("tok", "hd"), None),
            P(("tok", "hd"), None),
            P(("tok", "hd")),
            P(("tok", "hd")),
        ),
        out_specs=(
            P(("tok", "hd"), None),
            P(("tok", "hd"), None),
            P(("tok", "hd"), None),
            P(("tok", "hd"), None),
            P(("tok", "hd"), None),
            P(("tok", "hd"), None),
            P(None, ("tok", "hd")),
        ),
        check_vma=False,
    )
```

profile of v0, /device:TPU:0, one launch (start us, length us, event | category | flops | bytes accessed | tf_op | source)
XLA Modules:
  0.0 732.9 jit_solution(1573320555635671999)
XLA Ops:
  21.4 43.4 %all-gather.1 = bf16[32,24,2]{1,2,0:T(2,128)(2,1)S(1)} all-gather(bf16[1,24,2]{1,2,0:T(2,128)(2,1)} %bitcast.176), channel_id=1, replica_groups=mesh['tok'=16,'hd'=2] {'tok','hd'}, dimensions={0}, use_global_device_ids=true | all-gather | bytes 3168 | tf_op jit(solution)/shard_map/all_gather | solution.py:155
  73.7 4.1 fusion.125
  98.8 4.2 add_convert_fusion.4
  105.9 5.8 all_to_all.63
  113.1 25.3 %while.27 = (s32[]{:T(128)}, bf16[2,512,6,64]{1,3,2,0:T(8,128)(2,1)S(1)}, f32[2,6,512]{2,1,0:T(8,128)S(1)}, s32[2]{0:T(128)S(1)}, s32[1024]{0:T(1024)S(1)}, /*in...) while((s32[]{:T(128)}, ...), condition=%wide.region_7.8_spmd, body=%wide.region_4.7_spmd.sunk | while | flops 845870592 | bytes 42341076 | solution.py:89
  121.3 4.4 fusion.180
  130.3 3.6 fusion.179
  133.9 4.4 fusion.180
  147.5 5.8 all_to_all.64
  163.8 27.4 %all-gather.11.cloned.1.call-done = bf16[2304,768]{1,0:T(8,128)(2,1)} async-done(((bf16[72,768]{1,0:T(8,128)(2,1)}), bf16[2304,768]{1,0:T(8,128)(2,1)}) %all-gather.11.cloned.1.call-update) | async-done | bytes 3538960 | tf_op jit(solution)/shard_map/all_gather | solution.py:153
  191.2 6.8 fusion.128
  197.9 50.2 %all-gather.13.cloned.1.call-done = bf16[768,1152]{1,0:T(8,128)(2,1)} async-done(((bf16[24,1152]{1,0:T(8,128)(2,1)}), bf16[768,1152]{1,0:T(8,128)(2,1)}) %all-gather.13.cloned.1.call-update) | async-done | bytes 1769488 | tf_op jit(solution)/shard_map/all_gather | solution.py:154
  248.1 9.0 %add_convert_fusion = (bf16[512,1152]{1,0:T(8,128)(2,1)S(1)}, f32[512,1152]{1,0:T(8,128)S(1)}, f32[512,1152]{1,0:T(8,128)S(1)}) fusion(f32[512,2304]{1,0:T(8,128)} %fusion.128, bf16[768,1152]{1,0:T(8,128)(2,1)} %all-gather.13.cloned.1.call-done, bf16[512,768]{1,0:T(8,128)(2,1)S(1)} %copy-done.8, f32[512]{0:T(512)S(1)} %copy-done.32), kind=kOutput, calls=%fused_computation.82 | convolution fusion | flops 950206464 | bytes 13174784 | tf_op jit(solution)/shard_map/dot_general | solution.py:55
  268.9 4.3 fusion.107
  273.3 7.2 fusion.103
  283.8 4.4 all_to_all.65
  294.3 145.9 %while.28 = (s32[]{:T(128)}, f32[1024,6,64]{0,2,1:T(8,128)}, f32[1024,6,64]{0,2,1:T(8,128)}, bf16[2,512,6,64]{1,3,2,0:T(8,128)(2,1)}, s32[2]{0:T(128)S(1)}, /*in...) while((s32[]{:T(128)}, f32[1024,6,64]{0,2,1:T(8,128)}, ...), condition=%wide.region_14.15_spmd.clone, body=%wide.region_12.14_spmd.clone.sunk | while | flops 2100044288 | bytes 205775664 | solution.py:130
  298.3 5.0 bitcast_add_fusion.7
  303.3 6.3 fusion.191
  309.6 27.1 %fusion.194 = bf16[2,512,6,64]{1,3,2,0:T(8,128)(2,1)} fusion(bf16[2,512,6,64]{1,3,2,0:T(8,128)(2,1)} %get-tuple-element.481, s32[]{:T(128)S(6)} %copy.130, bf16[1024,6,64]{0,2,1:T(8,128)(2,1)S(1)} %get-tuple-element.502, f32[6,512,1024]{2,1,0:T(8,128)} %fusion.191, f32[6,512,1024]{2,1,0:T(8,128)} %copy-done, ...), kind=kOutput, calls=%fused_computation.45.clone.1 | convolution fusion | flops 437653504 | bytes 52592644 | tf_op jit(solution)/shard_map/while/body/eval_jaxpr/hqk,khd->qhd/dot_general | solution.py:113
  336.7 29.5 %bitcast_add_fusion.6 = f32[1024,6,64]{0,2,1:T(8,128)} fusion(f32[1024,6,64]{0,2,1:T(8,128)} %get-tuple-element.479, f32[6,512,1024]{2,1,0:T(8,128)} %fusion.191, f32[6,512,1024]{2,1,0:T(8,128)} %copy-done, f32[6,512]{1,0:T(8,128)S(1)} %dynamic-slice_bitcast_fusion.2, pred[512,1024]{1,0:T(8,128)(4,1)S(1)} %fusion.193, pred[]{:T(512)S(6)} %compare.3, ...), kind=kOutput, calls=%fused_computation.41.clone.1 | convolution fusion | flops 438439936 | bytes 54951940 | tf_op jit(solution)/shard_map/while/body/eval_jaxpr/hqk,qhd->khd/dot_general | solution.py:118
  370.1 6.5 bitcast_add_fusion.7
  376.6 6.3 fusion.191
  382.9 27.3 %fusion.194 = bf16[2,512,6,64]{1,3,2,0:T(8,128)(2,1)} fusion(bf16[2,512,6,64]{1,3,2,0:T(8,128)(2,1)} %get-tuple-element.481, s32[]{:T(128)S(6)} %copy.130, bf16[1024,6,64]{0,2,1:T(8,128)(2,1)S(1)} %get-tuple-element.502, f32[6,512,1024]{2,1,0:T(8,128)} %fusion.191, f32[6,512,1024]{2,1,0:T(8,128)} %copy-done, ...), kind=kOutput, calls=%fused_computation.45.clone.1 | convolution fusion | flops 437653504 | bytes 52592644 | tf_op jit(solution)/shard_map/while/body/eval_jaxpr/hqk,khd->qhd/dot_general | solution.py:113
  410.2 29.8 %bitcast_add_fusion.6 = f32[1024,6,64]{0,2,1:T(8,128)} fusion(f32[1024,6,64]{0,2,1:T(8,128)} %get-tuple-element.479, f32[6,512,1024]{2,1,0:T(8,128)} %fusion.191, f32[6,512,1024]{2,1,0:T(8,128)} %copy-done, f32[6,512]{1,0:T(8,128)S(1)} %dynamic-slice_bitcast_fusion.2, pred[512,1024]{1,0:T(8,128)(4,1)S(1)} %fusion.193, pred[]{:T(512)S(6)} %compare.3, ...), kind=kOutput, calls=%fused_computation.41.clone.1 | convolution fusion | flops 438439936 | bytes 54951940 | tf_op jit(solution)/shard_map/while/body/eval_jaxpr/hqk,qhd->khd/dot_general | solution.py:118
  446.2 4.9 copy.103
  451.1 6.3 all_to_all.66
  466.3 5.1 fusion.105
  473.0 4.2 fusion.100
  479.3 38.3 %all-reduce.2 = f32[2,768]{1,0:T(2,128)S(1)} all-reduce(f32[2,768]{1,0:T(2,128)S(1)} %pad_maximum_fusion.8), channel_id=6, replica_groups=mesh['tok'=16,'hd'=2] {'tok','hd'}, use_global_device_ids=true, to_apply=%region_23.24.clone | all-reduce | flops 1536 | bytes 12288
  526.7 73.3 %reduce-scatter.12.cloned.1.call-done = f32[72,768]{1,0:T(8,128)} async-done(((f32[2304,768]{1,0:T(8,128)}), f32[72,768]{1,0:T(8,128)}) %reduce-scatter.12.cloned.1.call-update) | async-done | bytes 221200 | tf_op jit(solution)/shard_map/reduce_scatter | solution.py:270
  601.6 122.6 %reduce-scatter.8.cloned.1.call-done = f32[72,768]{1,0:T(8,128)} async-done(((f32[2304,768]{1,0:T(8,128)}), f32[72,768]{1,0:T(8,128)}) %reduce-scatter.8.cloned.1.call-update) | async-done | bytes 221200 | tf_op jit(solution)/shard_map/reduce_scatter | solution.py:268
  (252 shorter events, 136.7 us)
Async XLA Ops:
  7.2 66.5 %all-gather.7.cloned.1.call-start = ((), (), s32[]{:S(2)}) async-start(), calls=%async_computation.8 | async-start | bytes 3649536 | tf_op jit(solution)/shard_map/all_gather | solution.py:151
  7.9 151.9 %all-gather.9.cloned.1.call-start = ((), (), s32[]{:S(2)}) async-start(), calls=%async_computation.9 | async-start | bytes 1216512 | tf_op jit(solution)/shard_map/all_gather | solution.py:152
  8.6 182.5 %all-gather.11.cloned.1.call-start = ((), (), s32[]{:S(2)}) async-start(), calls=%async_computation.10 | async-start | bytes 3649536 | tf_op jit(solution)/shard_map/all_gather | solution.py:153
  9.4 238.7 %all-gather.13.cloned.1.call-start = ((), (), s32[]{:S(2)}) async-start(), calls=%async_computation.11 | async-start | bytes 1824768 | tf_op jit(solution)/shard_map/all_gather | solution.py:154
  10.0 513.7 %reduce-scatter.10.cloned.1.call-start = ((), (), s32[]{:S(2)}) async-start(), calls=%async_computation.13 | async-start | bytes 2433024 | tf_op jit(solution)/shard_map/reduce_scatter | solution.py:269
  17.1 56.6 %copy-start.34 = (f32[512]{0:T(512)}, f32[512]{0:T(512)S(1)}, u32[]{:S(2)}) copy-start(f32[512]{0:T(512)S(1)} %broadcast_multiply_fusion.6) | copy-start | bytes 6148
  18.6 51.2 %copy-start.40 = (f32[512]{0:T(512)}, f32[512]{0:T(512)S(1)}, u32[]{:S(2)}) copy-start(f32[512]{0:T(512)S(1)} %fusion.99) | copy-start | bytes 6148
  18.6 55.0 %copy-start.36 = (f32[512]{0:T(512)}, f32[512]{0:T(512)S(1)}, u32[]{:S(2)}) copy-start(f32[512]{0:T(512)S(1)} %fusion.118) | copy-start | bytes 6148
  65.5 8.2 %copy-start.30 = (f32[768]{0:T(1024)}, f32[768]{0:T(1024)S(1)}, u32[]{:S(2)}) copy-start(f32[768]{0:T(1024)S(1)} %get-tuple-element.201) | copy-start | bytes 9220
  66.5 7.2 copy-start.3
  155.0 4.8 copy-start.4
  155.0 4.8 copy-start.32
  159.8 31.4 %copy-start.42 = (f32[768]{0:T(1024)S(1)}, f32[768]{0:T(1024)}, u32[]{:S(2)}) copy-start(f32[768]{0:T(1024)} %get-tuple-element.200) | copy-start | bytes 9220
  191.1 57.0 %copy-start.8 = (bf16[512,768]{1,0:T(8,128)(2,1)S(1)}, bf16[512,768]{1,0:T(8,128)(2,1)}, u32[]{:S(2)}) copy-start(bf16[512,768]{1,0:T(8,128)(2,1)} %param.19) | copy-start | bytes 2359300
  248.1 9.0 %copy-start.15 = (f32[512,2304]{1,0:T(8,128)S(1)}, f32[512,2304]{1,0:T(8,128)}, u32[]{:S(2)}) copy-start(f32[512,2304]{1,0:T(8,128)} %fusion.128) | copy-start | bytes 14155780
  257.1 3.7 copy-start.44
  258.7 4.9 copy-start.20
  268.8 256.3 %reduce-scatter.14.cloned.1.call-start = ((), (), s32[]{:S(2)}) async-start(), calls=%async_computation.15 | async-start | bytes 3649536
  273.2 326.7 %reduce-scatter.12.cloned.1.call-start = ((), (), s32[]{:S(2)}) async-start(), calls=%async_computation.14 | async-start | bytes 7299072 | tf_op jit(solution)/shard_map/reduce_scatter | solution.py:270
  280.6 443.6 %reduce-scatter.8.cloned.1.call-start = ((), (), s32[]{:S(2)}) async-start(), calls=%async_computation.12 | async-start | bytes 7299072 | tf_op jit(solution)/shard_map/reduce_scatter | solution.py:268
  298.3 5.0 copy-start
  370.1 6.5 copy-start
  440.2 2.6 copy-start.19
  462.4 2.7 copy-start.23
  473.0 4.3 copy-start.41
  477.3 41.0 %copy-start.2 = (f32[512,768]{1,0:T(8,128)S(1)}, f32[512,768]{1,0:T(8,128)}, u32[]{:S(2)}) copy-start(f32[512,768]{1,0:T(8,128)} %copy-done.1) | copy-start | bytes 4718596
  477.3 40.9 %copy-start.9 = (bf16[512,768]{1,0:T(8,128)(2,1)S(1)}, bf16[512,768]{1,0:T(8,128)(2,1)}, u32[]{:S(2)}) copy-start(bf16[512,768]{1,0:T(8,128)(2,1)} %param.19) | copy-start | bytes 2359300
  477.3 40.9 %copy-start.39 = (f32[512]{0:T(512)S(1)}, f32[512]{0:T(512)}, u32[]{:S(2)}) copy-start(f32[512]{0:T(512)} %copy-done.38) | copy-start | bytes 6148
  518.2 3.2 copy-start.12
  518.2 3.2 copy-start.14
  518.3 3.2 copy-start.33
  518.3 3.2 copy-start.45
  (25 other events, 36.2 us)
Sparse Core Ops, SparseCore 0:
  10.9 62.7 all-gather.6
  76.6 52.7 all-gather.8
  132.2 58.8 all-gather.10
  193.8 54.2 all-gather.12
  269.0 98.8 reduce-scatter.9
  373.2 102.4 reduce-scatter.13
  481.3 118.5 reduce-scatter.11
  605.6 118.4 reduce-scatter.7
where the time goes:
time: 742 us; the launch traced here: 733 us
  waiting for transfers between devices  279 us (38%)
  matrix products  208 us (28%)
  blocking collectives  108 us (15%)
  local copies, waits for them, and re-layouts  72.7 us (10%)
  other arithmetic  47 us (6%)
  between operations  15.7 us (2%)
    reduce_scatter x1, waiting for transfers between devices, per_device(): lax.psum_scatter(qkv_term, ('tok', 'hd'), scatter_dimension=0, tiled=True)  123 us
    reduce_scatter x1, waiting for transfers between devices, per_device(): lax.psum_scatter(in_term, ('tok', 'hd'), scatter_dimension=0, tiled=True)  73.3 us
    dot_general x2, matrix products, one_block(): jnp.einsum('hqk,qhd->khd', grad_scores, query_block, preferred_element_ty...  59.3 us
    dot_general x2, matrix products, one_block(): jnp.einsum('hqk,khd->qhd', grad_scores, keys, preferred_element_type=jnp....  54.3 us
    all_gather x1, waiting for transfers between devices, per_device(): lax.all_gather(w_down, ('tok', 'hd'), axis=0, tiled=True)  50.2 us
    all_gather x1, blocking collectives, per_device(): lax.all_gather(norm_gains, ('tok', 'hd'), axis=1, tiled=True)  43.4 us
    unnamed x2, blocking collectives  40.3 us
    all_gather x1, waiting for transfers between devices, per_device(): lax.all_gather(w_in, ('tok', 'hd'), axis=0, tiled=True)  27.4 us
  transfers between devices with their start and end apart: 8, of which 5 were waited for; matrix products, arithmetic and copies ran while one was open for 40% of the time, Pallas kernels for 0%

commit v1 on v0

--- a/solution.py
+++ b/solution.py
@@ -9,6 +9,12 @@
 EPS = 1e-05
 THETA = 160000.0
 NEG = -1e30
+
+
+def tiled_gather(x, axis, dim):
+    peers = lax.axis_size(axis)
+    repeats = [peers if d == dim else 1 for d in range(x.ndim)]
+    return lax.all_to_all(jnp.tile(x, repeats), axis, split_axis=dim, concat_axis=dim, tiled=True)
 
 
 def layer_norm(row_values, gain):
@@ -151,7 +157,7 @@
         lax.all_gather(w_qkv, ("tok", "hd"), axis=0, tiled=True),
         lax.all_gather(w_attn_out, ("tok", "hd"), axis=0, tiled=True),
         lax.all_gather(w_in, ("tok", "hd"), axis=0, tiled=True),
-        lax.all_gather(w_down, ("tok", "hd"), axis=0, tiled=True),
+        tiled_gather(w_down, ("tok", "hd"), 0),
         lax.all_gather(norm_gains, ("tok", "hd"), axis=1, tiled=True),
     )
     full_qkv, full_attn_out, full_in, full_down, full_gains = gathered

time: 742 us -> 742 us (level)
  waiting for transfers between devices: 279 us -> 234 us
  blocking collectives: 108 us -> 131 us
  matrix products: 208 us -> 226 us
    reduce_scatter x1, waiting for transfers between devices: 73.3 us -> 27.5 us  [per_device(): lax.psum_scatter(in_term, ('tok', 'hd'), scatter_dimension=0, tiled=True)]
    unnamed x2, blocking collectives: 40.3 us -> 63.4 us
    dot_general x4, matrix products: 8.51 us -> 17.6 us  [block_scores(): jnp.einsum('qhd,khd->hqk', query_block, keys, preferred_element_type=jnp....]
    dot_general x2, matrix products: 11.5 us -> 19 us  [one_block(): jnp.einsum('hqk,qhd->khd', probs_low, grad_block, preferred_element_type=...]
    unnamed x98 -> x100, local copies, waits for them, and re-layouts: 22.2 us -> 21 us
  transfers between devices with their start and end apart: 8 -> 9, of which waited for: 5 -> 5; matrix products, arithmetic and copies ran while one was open for 40% -> 43% of each run, Pallas kernels for 0% -> 0%
where the time goes in v1:
time: 742 us; the launch traced here: 734 us
  waiting for transfers between devices  234 us (32%)
  matrix products  226 us (30%)
  blocking collectives  131 us (18%)
  local copies, waits for them, and re-layouts  74.4 us (10%)
  other arithmetic  44.7 us (6%)
  between operations  15.9 us (2%)
    reduce_scatter x1, waiting for transfers between devices, per_device(): lax.psum_scatter(qkv_term, ('tok', 'hd'), scatter_dimension=0, tiled=True)  123 us
    unnamed x2, blocking collectives  63.4 us
    dot_general x2, matrix products, one_block(): jnp.einsum('hqk,qhd->khd', grad_scores, query_block, preferred_element_ty...  59.4 us
    dot_general x2, matrix products, one_block(): jnp.einsum('hqk,khd->qhd', grad_scores, keys, preferred_element_type=jnp....  54.1 us
    all_gather x1, waiting for transfers between devices, per_device(): lax.all_gather(w_down, ('tok', 'hd'), axis=0, tiled=True)  50.2 us
    all_gather x1, blocking collectives, per_device(): lax.all_gather(norm_gains, ('tok', 'hd'), axis=1, tiled=True)  43.6 us
    all_gather x1, waiting for transfers between devices, per_device(): lax.all_gather(w_in, ('tok', 'hd'), axis=0, tiled=True)  27.8 us
    reduce_scatter x1, waiting for transfers between devices, per_device(): lax.psum_scatter(in_term, ('tok', 'hd'), scatter_dimension=0, tiled=True)  27.5 us
  transfers between devices with their start and end apart: 9, of which 5 were waited for; matrix products, arithmetic and copies ran while one was open for 43% of the time, Pallas kernels for 0%

profile of v1, /device:TPU:0, one launch (start us, length us, event | category | flops | bytes accessed | tf_op | source)
XLA Modules:
  0.0 733.6 jit_solution(16457114319937073787)
XLA Ops:
  12.9 43.6 %all-gather.1 = bf16[32,24,2]{1,2,0:T(2,128)(2,1)S(1)} all-gather(bf16[1,24,2]{1,2,0:T(2,128)(2,1)} %bitcast.177), channel_id=1, replica_groups=mesh['tok'=16,'hd'=2] {'tok','hd'}, dimensions={0}, use_global_device_ids=true | all-gather | bytes 3168 | tf_op jit(solution)/shard_map/all_gather | solution.py:161
  105.3 5.8 all_to_all.72
  112.6 25.3 %while.27 = (s32[]{:T(128)}, bf16[2,512,6,64]{1,3,2,0:T(8,128)(2,1)S(1)}, f32[2,6,512]{2,1,0:T(8,128)S(1)}, s32[2]{0:T(128)S(1)}, s32[1024]{0:T(1024)S(1)}, /*in...) while((s32[]{:T(128)}, ...), condition=%wide.region_7.8_spmd, body=%wide.region_4.7_spmd.sunk | while | flops 845870592 | bytes 42341068 | solution.py:95
  120.8 4.4 fusion.180
  133.4 4.4 fusion.180
  147.0 5.9 all_to_all.73
  163.3 27.8 %all-gather.11.cloned.1.call-done = bf16[2304,768]{1,0:T(8,128)(2,1)} async-done(((bf16[72,768]{1,0:T(8,128)(2,1)}), bf16[2304,768]{1,0:T(8,128)(2,1)}) %all-gather.11.cloned.1.call-update) | async-done | bytes 3538960 | tf_op jit(solution)/shard_map/all_gather | solution.py:159
  191.1 6.8 fusion.128
  197.9 50.2 %all-gather.13.cloned.1.call-done = bf16[768,1152]{1,0:T(8,128)(2,1)} async-done(((bf16[24,1152]{1,0:T(8,128)(2,1)}), bf16[768,1152]{1,0:T(8,128)(2,1)}) %all-gather.13.cloned.1.call-update) | async-done | bytes 1769488 | tf_op jit(solution)/shard_map/all_gather | solution.py:210
  248.0 9.0 %add_convert_fusion = (bf16[512,1152]{1,0:T(8,128)(2,1)S(1)}, f32[512,1152]{1,0:T(8,128)S(1)}, f32[512,1152]{1,0:T(8,128)S(1)}) fusion(f32[512,2304]{1,0:T(8,128)} %fusion.128, bf16[768,1152]{1,0:T(8,128)(2,1)} %all-gather.13.cloned.1.call-done, bf16[512,768]{1,0:T(8,128)(2,1)S(1)} %copy-done.7, f32[512]{0:T(512)S(1)} %copy-done.32), kind=kOutput, calls=%fused_computation.82 | convolution fusion | flops 950206464 | bytes 13174784 | tf_op jit(solution)/shard_map/dot_general | solution.py:61
  268.8 4.3 fusion.107
  273.3 7.2 fusion.103
  283.8 4.4 all_to_all.74
  294.2 162.8 %while.28 = (s32[]{:T(128)}, f32[1024,6,64]{0,2,1:T(8,128)}, f32[1024,6,64]{0,2,1:T(8,128)}, bf16[2,512,6,64]{1,3,2,0:T(8,128)(2,1)}, s32[2]{0:T(128)S(1)}, /*in...) while((s32[]{:T(128)}, f32[1024,6,64]{0,2,1:T(8,128)}, ...), condition=%wide.region_14.15_spmd.clone, body=%wide.region_12.14_spmd.clone.sunk | while | flops 2100044288 | bytes 155440416 | solution.py:136
  296.6 6.4 fusion.192
  303.0 6.3 fusion.191
  309.3 29.6 %bitcast_add_fusion.6 = f32[1024,6,64]{0,2,1:T(8,128)} fusion(f32[1024,6,64]{0,2,1:T(8,128)} %get-tuple-element.479, f32[6,512,1024]{2,1,0:T(8,128)} %fusion.191, f32[6,512,1024]{2,1,0:T(8,128)} %fusion.192, f32[6,512]{1,0:T(8,128)S(1)} %dynamic-slice_bitcast_fusion.2, pred[512,1024]{1,0:T(8,128)(4,1)S(1)} %fusion.193, pred[]{:T(512)S(6)} %compare.3, ...), kind=kOutput, calls=%fused_computation.41.clone.1 | convolution fusion | flops 438439936 | bytes 54951940 | tf_op jit(solution)/shard_map/while/body/eval_jaxpr/hqk,qhd->khd/dot_general | solution.py:124
  338.9 26.9 %fusion.194 = bf16[2,512,6,64]{1,3,2,0:T(8,128)(2,1)} fusion(bf16[2,512,6,64]{1,3,2,0:T(8,128)(2,1)} %get-tuple-element.481, s32[]{:T(128)} %get-tuple-element.478, bf16[1024,6,64]{0,2,1:T(8,128)(2,1)S(1)} %get-tuple-element.502, f32[6,512,1024]{2,1,0:T(8,128)} %fusion.191, f32[6,512,1024]{2,1,0:T(8,128)} %fusion.192, ...), kind=kOutput, calls=%fused_computation.45.clone.1 | convolution fusion | flops 437653504 | bytes 52593152 | tf_op jit(solution)/shard_map/while/body/eval_jaxpr/hqk,khd->qhd/dot_general | solution.py:119
  365.8 9.3 %bitcast_add_fusion.7 = f32[1024,6,64]{0,2,1:T(8,128)} fusion(f32[1024,6,64]{0,2,1:T(8,128)} %get-tuple-element.480, f32[6,512,1024]{2,1,0:T(8,128)} %fusion.192, f32[6,512]{1,0:T(8,128)S(1)} %dynamic-slice_bitcast_fusion.2, pred[512,1024]{1,0:T(8,128)(4,1)S(1)} %fusion.193, pred[]{:T(512)S(6)} %compare.3, ...), kind=kOutput, calls=%fused_computation.40.clone.1 | convolution fusion | flops 416022528 | bytes 16658437 | tf_op jit(solution)/shard_map/while/body/eval_jaxpr/hqk,qhd->khd/dot_general | solution.py:129
  377.3 6.4 fusion.192
  383.7 6.3 fusion.191
  390.0 29.8 %bitcast_add_fusion.6 = f32[1024,6,64]{0,2,1:T(8,128)} fusion(f32[1024,6,64]{0,2,1:T(8,128)} %get-tuple-element.479, f32[6,512,1024]{2,1,0:T(8,128)} %fusion.191, f32[6,512,1024]{2,1,0:T(8,128)} %fusion.192, f32[6,512]{1,0:T(8,128)S(1)} %dynamic-slice_bitcast_fusion.2, pred[512,1024]{1,0:T(8,128)(4,1)S(1)} %fusion.193, pred[]{:T(512)S(6)} %compare.3, ...), kind=kOutput, calls=%fused_computation.41.clone.1 | convolution fusion | flops 438439936 | bytes 54951940 | tf_op jit(solution)/shard_map/while/body/eval_jaxpr/hqk,qhd->khd/dot_general | solution.py:124
  419.8 27.3 %fusion.194 = bf16[2,512,6,64]{1,3,2,0:T(8,128)(2,1)} fusion(bf16[2,512,6,64]{1,3,2,0:T(8,128)(2,1)} %get-tuple-element.481, s32[]{:T(128)} %get-tuple-element.478, bf16[1024,6,64]{0,2,1:T(8,128)(2,1)S(1)} %get-tuple-element.502, f32[6,512,1024]{2,1,0:T(8,128)} %fusion.191, f32[6,512,1024]{2,1,0:T(8,128)} %fusion.192, ...), kind=kOutput, calls=%fused_computation.45.clone.1 | convolution fusion | flops 437653504 | bytes 52593152 | tf_op jit(solution)/shard_map/while/body/eval_jaxpr/hqk,khd->qhd/dot_general | solution.py:119
  447.1 9.7 %bitcast_add_fusion.7 = f32[1024,6,64]{0,2,1:T(8,128)} fusion(f32[1024,6,64]{0,2,1:T(8,128)} %get-tuple-element.480, f32[6,512,1024]{2,1,0:T(8,128)} %fusion.192, f32[6,512]{1,0:T(8,128)S(1)} %dynamic-slice_bitcast_fusion.2, pred[512,1024]{1,0:T(8,128)(4,1)S(1)} %fusion.193, pred[]{:T(512)S(6)} %compare.3, ...), kind=kOutput, calls=%fused_computation.40.clone.1 | convolution fusion | flops 416022528 | bytes 16658437 | tf_op jit(solution)/shard_map/while/body/eval_jaxpr/hqk,qhd->khd/dot_general | solution.py:129
  462.8 4.9 copy.103
  467.7 6.3 all_to_all.75
  482.9 5.1 fusion.105
  494.0 4.4 fusion.100
  500.3 61.5 %all-reduce.2 = f32[2,768]{1,0:T(2,128)S(1)} all-reduce(f32[2,768]{1,0:T(2,128)S(1)} %pad_maximum_fusion.8), channel_id=6, replica_groups=mesh['tok'=16,'hd'=2] {'tok','hd'}, use_global_device_ids=true, to_apply=%region_23.24.clone | all-reduce | flops 1536 | bytes 12288
  565.5 4.4 add_convert_fusion.2
  573.0 27.5 %reduce-scatter.12.cloned.1.call-done = f32[72,768]{1,0:T(8,128)} async-done(((f32[2304,768]{1,0:T(8,128)}), f32[72,768]{1,0:T(8,128)}) %reduce-scatter.12.cloned.1.call-update) | async-done | bytes 221200 | tf_op jit(solution)/shard_map/reduce_scatter | solution.py:276
  602.2 122.6 %reduce-scatter.8.cloned.1.call-done = f32[72,768]{1,0:T(8,128)} async-done(((f32[2304,768]{1,0:T(8,128)}), f32[72,768]{1,0:T(8,128)}) %reduce-scatter.8.cloned.1.call-update) | async-done | bytes 221200 | tf_op jit(solution)/shard_map/reduce_scatter | solution.py:274
  (253 shorter events, 146.2 us)
Async XLA Ops:
  7.2 54.4 %copy-start.45 = (u32[32]{0:T(128)S(1)}, u32[32]{0:T(128)}, u32[]{:S(2)}) copy-start(u32[32]{0:T(128)} %constant.163) | copy-start | bytes 388
  7.2 66.5 %all-gather.7.cloned.1.call-start = ((), (), s32[]{:S(2)}) async-start(), calls=%async_computation.9 | async-start | bytes 3649536 | tf_op jit(solution)/shard_map/all_gather | solution.py:157
  7.9 151.4 %all-gather.9.cloned.1.call-start = ((), (), s32[]{:S(2)}) async-start(), calls=%async_computation.10 | async-start | bytes 1216512 | tf_op jit(solution)/shard_map/all_gather | solution.py:158
  8.7 182.4 %all-gather.11.cloned.1.call-start = ((), (), s32[]{:S(2)}) async-start(), calls=%async_computation.11 | async-start | bytes 3649536 | tf_op jit(solution)/shard_map/all_gather | solution.py:159
  9.4 238.6 %all-gather.13.cloned.1.call-start = ((), (), s32[]{:S(2)}) async-start(), calls=%async_computation.12 | async-start | bytes 1824768 | tf_op jit(solution)/shard_map/all_gather | solution.py:210
  10.0 560.0 %reduce-scatter.10.cloned.1.call-start = ((), (), s32[]{:S(2)}) async-start(), calls=%async_computation.14 | async-start | bytes 2433024 | tf_op jit(solution)/shard_map/reduce_scatter | solution.py:275
  11.4 62.3 %copy-start.34 = (f32[512]{0:T(512)}, f32[512]{0:T(512)S(1)}, u32[]{:S(2)}) copy-start(f32[512]{0:T(512)S(1)} %broadcast_multiply_fusion.6) | copy-start | bytes 6148
  12.9 43.6 %copy-start.40 = (f32[512]{0:T(512)}, f32[512]{0:T(512)S(1)}, u32[]{:S(2)}) copy-start(f32[512]{0:T(512)S(1)} %fusion.99) | copy-start | bytes 6148
  12.9 60.8 %copy-start.36 = (f32[512]{0:T(512)}, f32[512]{0:T(512)S(1)}, u32[]{:S(2)}) copy-start(f32[512]{0:T(512)S(1)} %fusion.118) | copy-start | bytes 6148
  57.2 16.5 %copy-start.30 = (f32[768]{0:T(1024)}, f32[768]{0:T(1024)S(1)}, u32[]{:S(2)}) copy-start(f32[768]{0:T(1024)S(1)} %get-tuple-element.201) | copy-start | bytes 9220
  61.0 3.4 copy-start.20
  63.0 10.7 %copy-start.2 = (bf16[512,768]{1,0:T(8,128)(2,1)S(1)}, bf16[512,768]{1,0:T(8,128)(2,1)}, u32[]{:S(2)}) copy-start(bf16[512,768]{1,0:T(8,128)(2,1)} %param.13) | copy-start | bytes 2359300
  154.5 4.8 copy-start.3
  154.5 4.8 copy-start.32
  159.3 31.8 %copy-start.42 = (f32[768]{0:T(1024)S(1)}, f32[768]{0:T(1024)}, u32[]{:S(2)}) copy-start(f32[768]{0:T(1024)} %get-tuple-element.200) | copy-start | bytes 9220
  191.1 57.0 %copy-start.7 = (bf16[512,768]{1,0:T(8,128)(2,1)S(1)}, bf16[512,768]{1,0:T(8,128)(2,1)}, u32[]{:S(2)}) copy-start(bf16[512,768]{1,0:T(8,128)(2,1)} %param.19) | copy-start | bytes 2359300
  248.0 9.0 %copy-start.12 = (f32[512,2304]{1,0:T(8,128)S(1)}, f32[512,2304]{1,0:T(8,128)}, u32[]{:S(2)}) copy-start(f32[512,2304]{1,0:T(8,128)} %fusion.128) | copy-start | bytes 14155780
  257.1 3.7 copy-start.44
  258.7 4.9 copy-start.19
  268.8 302.7 %reduce-scatter.14.cloned.1.call-start = ((), (), s32[]{:S(2)}) async-start(), calls=%async_computation.16 | async-start | bytes 3649536
  273.2 327.4 %reduce-scatter.12.cloned.1.call-start = ((), (), s32[]{:S(2)}) async-start(), calls=%async_computation.15 | async-start | bytes 7299072 | tf_op jit(solution)/shard_map/reduce_scatter | solution.py:276
  280.5 444.2 %reduce-scatter.8.cloned.1.call-start = ((), (), s32[]{:S(2)}) async-start(), calls=%async_computation.13 | async-start | bytes 7299072 | tf_op jit(solution)/shard_map/reduce_scatter | solution.py:274
  296.6 6.4 copy-start.6
  377.3 6.4 copy-start.6
  488.8 5.1 copy-start.23
  488.8 5.1 copy-start.25
  488.8 5.1 copy-start.27
  490.2 75.4 %all-to-all-start.2 = ((bf16[32,24,1152]{2,1,0:T(8,128)(2,1)}), bf16[32,24,1152]{2,1,0:T(8,128)(2,1)}, u32[]{:S(2)}, u32[]{:S(2)}) async-start(bf16[32,24,1152]{2,1,0:T(8,128)(2,1)} %tile.2), calls=%async_computation.2 | async-start | bytes 3538944 | tf_op jit(solution)/shard_map/all_to_all | solution.py:17
  494.0 4.4 copy-start.41
  498.3 64.2 %copy-start.1 = (f32[512,768]{1,0:T(8,128)S(1)}, f32[512,768]{1,0:T(8,128)}, u32[]{:S(2)}) copy-start(f32[512,768]{1,0:T(8,128)} %copy-done) | copy-start | bytes 4718596
  498.3 64.2 %copy-start.8 = (bf16[512,768]{1,0:T(8,128)(2,1)S(1)}, bf16[512,768]{1,0:T(8,128)(2,1)}, u32[]{:S(2)}) copy-start(bf16[512,768]{1,0:T(8,128)(2,1)} %param.19) | copy-start | bytes 2359300
  498.4 64.2 %copy-start.39 = (f32[512]{0:T(512)S(1)}, f32[512]{0:T(512)}, u32[]{:S(2)}) copy-start(f32[512]{0:T(512)} %copy-done.38) | copy-start | bytes 6148
  (25 other events, 42.3 us)
Sparse Core Ops, SparseCore 0:
  10.9 62.7 all-gather.6
  76.6 52.8 all-gather.8
  132.3 58.6 all-gather.10
  193.8 54.2 all-gather.12
  268.9 98.8 reduce-scatter.9
  373.1 102.4 reduce-scatter.13
  481.3 119.1 reduce-scatter.11
  606.2 118.4 reduce-scatter.7
